TPU v7x, 512 devices: a whole 4x8x8 slice. The times are simulated.
512 devices in a mesh: img: 8 (over y_lo, core), fsdp: 64 (over x, z, y_hi).
Axes of the slice: x: 4, y: 8 (y_hi: 2, y_lo: 4; y = y_hi * 4 + y_lo), z: 8, core: 2. Of those that a mesh axis runs over, the one named last changes fastest.
Arguments:
- text_states: bfloat16 [16384, 8192], P('fsdp')
- text_gain: float32 [8192], replicated, may hold values from 0.1 to 1.9
- vision: bfloat16 [8, 512, 8192], P('img', 'fsdp'), may hold values from -6 to 6
- q_weight: bfloat16 [8192, 4096], P('fsdp', 'img'), may hold values from -0.0625 to 0.0625
- k_weight: bfloat16 [8192, 1024], P('fsdp', 'img'), may hold values from -0.0625 to 0.0625
- v_weight: bfloat16 [8192, 1024], P('fsdp', 'img'), may hold values from -0.0625 to 0.0625
- q_gain: float32 [128], replicated, may hold values from 1 to 16
- k_gain: float32 [128], replicated, may hold values from 1 to 16
- owners: int32 [256, 4], P('fsdp'), may hold values from 0 to 7
- counts: int32 [256], P('fsdp'), may hold values from 0 to 4
- gate_value: float32 [1], replicated, may hold values from 0.3 to 1.5
Outputs:
- attended: bfloat16 [16384, 4096], P('fsdp', 'img')
All inputs are finite; a program needn't handle non-finite values.
Results may differ from a plain program's by a relative error of at most 0.025.
The roundings to bfloat16 on the way count: a program that leaves them out, or rounds other values in their place, can miss the bound.
Values may be sent and summed in bfloat16 or wider, within the bound.
No kernel may reach another device: no remote copies, remote signals or barrier semaphores. Data moves between devices by JAX's collectives and lax.ppermute only.
A program may use at most 64 MiB of HBM per device.

v0:
```python
import jax
import jax.numpy as jnp
from jax import lax
from jax.sharding import PartitionSpec as P

norm_epsilon = 1e-05
masked_score = -1e30


def head_norm(values, gain):
    mean_square = jnp.mean(values * values, axis=-1, keepdims=True)
    return values * lax.rsqrt(mean_square + norm_epsilon) * gain


def on_device(
    text_states,
    text_gain,
    vision,
    q_weight,
    k_weight,
    v_weight,
    q_gain,
    k_gain,
    owners,
    counts,
    gate_value,
):
    token_rows = text_states.shape[0]
    width = text_states.shape[1]
    head_size = q_gain.shape[0]
    per_group = q_weight.shape[1] // head_size
    images = lax.axis_size("img")
    shard_tokens = vision.shape[1]
    text_float = text_states.astype(jnp.float32)
    normed = (
        text_float
        * lax.rsqrt(jnp.mean(text_float * text_float, axis=-1, keepdims=True) + norm_epsilon)
        * text_gain
    ).astype(jnp.bfloat16)
    visual = lax.all_gather(vision, "img", axis=0, tiled=True).reshape(images * shard_tokens, width)
    columns = visual
    joined = jnp.concatenate(
        (
            lax.all_gather(k_weight, "fsdp", axis=0, tiled=True),
            lax.all_gather(v_weight, "fsdp", axis=0, tiled=True),
        ),
        axis=1,
    )
    pair_full = jnp.dot(columns, joined, preferred_element_type=jnp.float32)
    columns = normed
    query_full = jnp.dot(
        columns,
        lax.all_gather(q_weight, "fsdp", axis=0, tiled=True),
        preferred_element_type=jnp.float32,
    )
    row_count = token_rows * per_group
    queries = (
        head_norm(query_full.reshape(token_rows, per_group, head_size), q_gain)
        .astype(jnp.bfloat16)
        .reshape(row_count, head_size)
    )
    keys = (
        head_norm(pair_full[:, :head_size], k_gain)
        .astype(jnp.bfloat16)
        .reshape(images, shard_tokens, head_size)
    )
    values = pair_full[:, head_size:].astype(jnp.bfloat16).reshape(images, shard_tokens, head_size)
    block_count = owners.shape[0]
    live_slot = jnp.arange(owners.shape[1], dtype=jnp.int32)[None, :] < counts[:, None]
    matched = (
        owners[:, :, None] == jnp.arange(images, dtype=jnp.int32)[None, None, :]
    ) & live_slot[:, :, None]
    block_images = jnp.any(matched, axis=1)
    token_images = jnp.broadcast_to(
        block_images[:, None, :], (block_count, token_rows // block_count, images)
    ).reshape(token_rows, images)
    row_live = jnp.any(token_images, axis=1)
    score_scale = head_size ** (-0.5)
    key_piece = lax.all_gather(keys, "fsdp", axis=1, tiled=True)
    value_piece = lax.all_gather(values, "fsdp", axis=1, tiled=True)
    key_count = key_piece.shape[1]
    allowed = jnp.broadcast_to(token_images[:, :, None], (token_rows, images, key_count)).reshape(
        token_rows, images * key_count
    )
    running_max = jnp.full((row_count,), masked_score, jnp.float32)
    scores = (
        jnp.einsum(
            "rd,kd->rk",
            queries,
            key_piece.reshape(images * key_count, head_size),
            preferred_element_type=jnp.float32,
        )
        * score_scale
    )
    scores = jnp.where(
        allowed[:, None, :], scores.reshape(token_rows, per_group, -1), masked_score
    ).reshape(row_count, -1)
    new_max = jnp.maximum(running_max, jnp.max(scores, axis=1))
    weights = jnp.exp(scores - new_max[:, None]).astype(jnp.bfloat16)
    denominator = jnp.sum(weights.astype(jnp.float32), axis=1)
    numerator = jnp.dot(
        weights,
        value_piece.reshape(images * key_count, head_size),
        preferred_element_type=jnp.float32,
    )
    running_max, denominator, numerator = (new_max, denominator, numerator)
    live_rows = jnp.broadcast_to(row_live[:, None], (token_rows, per_group)).reshape(row_count)
    safe_denominator = jnp.where(live_rows, denominator, jnp.float32(1.0))
    factor = jnp.where(live_rows, jnp.tanh(gate_value[0]), jnp.float32(0.0))
    attended = numerator / safe_denominator[:, None] * factor[:, None]
    return attended.reshape(token_rows, per_group * head_size).astype(jnp.bfloat16)


def solution(mesh):
    in_specs = (
        P("fsdp", None),
        P(),
        P("img", "fsdp", None),
        P("fsdp", "img"),
        P("fsdp", "img"),
        P("fsdp", "img"),
        P(),
        P(),
        P("fsdp", None),
        P("fsdp"),
        P(),
    )
    out_specs = P("fsdp", "img")
    return jax.shard_map(
        on_device, mesh=mesh, in_specs=in_specs, out_specs=out_specs, check_vma=False
    )
```

profile of v0, /device:TPU:22, one launch (start us, length us, event | category | flops | bytes accessed | tf_op | source)
XLA Modules:
  0.0 737.3 jit_solution(17077881853206447943)
XLA Ops:
  6.5 0.7 all-gather.13.cloned.1.call-update
  7.3 0.7 all-gather.11.cloned.1.call-update
  8.1 0.7 all-gather.9.cloned.1.call-update
  8.8 0.5 all-gather.7.cloned.1.call-update
  9.4 38.2 %all-gather.13.cloned.1.call-done = bf16[8,8,8192]{2,1,0:T(8,128)(2,1)} async-done(((bf16[1,8,8192]{2,1,0:T(8,128)(2,1)}), bf16[8,8,8192]{2,1,0:T(8,128)(2,1)}) %all-gather.13.cloned.1.call-update) | async-done | bytes 1048592 | tf_op jit(solution)/shard_map/all_gather | solution.py:40
  47.6 143.9 %all-gather.11.cloned.1.call-done = bf16[8192,128]{1,0:T(8,128)(2,1)} async-done(((bf16[128,128]{1,0:T(8,128)(2,1)}), bf16[8192,128]{1,0:T(8,128)(2,1)}) %all-gather.11.cloned.1.call-update) | async-done | bytes 2097168 | tf_op jit(solution)/shard_map/all_gather | solution.py:45
  191.5 134.0 %all-gather.9.cloned.1.call-done = bf16[8192,128]{1,0:T(8,128)(2,1)} async-done(((bf16[128,128]{1,0:T(8,128)(2,1)}), bf16[8192,128]{1,0:T(8,128)(2,1)}) %all-gather.9.cloned.1.call-update) | async-done | bytes 2097168 | tf_op jit(solution)/shard_map/all_gather | solution.py:44
  325.5 3.3 fusion.14
  328.9 0.1 multiply_reduce_fusion
  329.0 1.3 fusion.20
  330.4 0.7 iota_compare_fusion.1
  331.2 0.9 fusion.23
  332.1 0.5 broadcast_in_dim.68
  332.6 0.8 copy.15
  333.3 5.7 broadcast_in_dim.70
  339.0 12.4 %broadcast_in_dim.71 = pred[1024,4096]{1,0:T(32,128)(4,1)} reshape(pred[256,4,4096]{2,1,0:T(4,128)(4,1)} %broadcast_in_dim.70) | data formatting | bytes 8388608 | tf_op jit(solution)/shard_map/jit(_where)/broadcast_in_dim | solution.py:95
  351.7 0.1 reshape.111
  352.5 3.1 fusion.1
  355.6 0.6 fusion.21
  356.3 156.7 %all-gather.7.cloned.1.call-done = bf16[8192,512]{1,0:T(8,128)(2,1)} async-done(((bf16[128,512]{1,0:T(8,128)(2,1)}), bf16[8192,512]{1,0:T(8,128)(2,1)}) %all-gather.7.cloned.1.call-update) | async-done | bytes 8388624 | tf_op jit(solution)/shard_map/all_gather | solution.py:53
  513.0 7.0 fusion.26
  520.0 0.2 mul.90
  520.2 0.3 reduce_sum.37
  520.6 0.3 mul.91
  520.9 0.1 fusion.19
  521.0 0.2 convert_element_type.32
  521.2 95.6 %all-gather.15.cloned.1.call-done = bf16[8,512,128]{2,1,0:T(8,128)(2,1)} async-done(((bf16[8,8,128]{2,1,0:T(8,128)(2,1)}), bf16[8,512,128]{2,1,0:T(8,128)(2,1)}) %all-gather.15.cloned.1.call-update) | async-done | bytes 1048592 | tf_op jit(solution)/shard_map/all_gather | solution.py:79
  616.8 6.0 fusion
  622.8 7.4 %convert_reduce_fusion = (f32[1024]{0:T(1024)S(1)}, bf16[1024,4096]{1,0:T(8,128)(2,1)}) fusion(f32[1024]{0:T(1024)S(1)} %broadcast_maximum_fusion, pred[1024,4096]{1,0:T(32,128)(4,1)S(1)} %copy-done.1, f32[1024,4096]{1,0:T(8,128)S(1)} %get-tuple-element.14), kind=kLoop, calls=%fused_computation | loop fusion | flops 25164800 | bytes 29368320 | tf_op jit(solution)/shard_map/reduce_sum | solution.py:100
  630.3 93.4 %all-gather.17.cloned.1.call-done = bf16[8,512,128]{2,1,0:T(8,128)(2,1)} async-done(((bf16[8,8,128]{2,1,0:T(8,128)(2,1)}), bf16[8,512,128]{2,1,0:T(8,128)(2,1)}) %all-gather.17.cloned.1.call-update) | async-done | bytes 1048592 | tf_op jit(solution)/shard_map/all_gather | solution.py:80
  723.7 5.9 fusion.13
  729.6 0.9 convert_element_type.37
  (24 shorter events, 0.6 us)
Async XLA Ops:
  6.5 349.1 %copy-start = (f32[128]{0:T(128)S(1)}, f32[128]{0:T(128)}, u32[]{:S(2)}) copy-start(f32[128]{0:T(128)} %param.17) | copy-start | bytes 1540
  6.5 41.0 %all-gather.13.cloned.1.call-start = ((), (), s32[]{:S(2)}) async-start(), calls=%async_computation.3 | async-start | bytes 1179648 | tf_op jit(solution)/shard_map/all_gather | solution.py:40
  7.3 184.2 %all-gather.11.cloned.1.call-start = ((), (), s32[]{:S(2)}) async-start(), calls=%async_computation.2 | async-start | bytes 2129920 | tf_op jit(solution)/shard_map/all_gather | solution.py:45
  8.0 317.5 %all-gather.9.cloned.1.call-start = ((), (), s32[]{:S(2)}) async-start(), calls=%async_computation.1 | async-start | bytes 2129920 | tf_op jit(solution)/shard_map/all_gather | solution.py:44
  8.7 504.2 %all-gather.7.cloned.1.call-start = ((), (), s32[]{:S(2)}) async-start(), calls=%async_computation | async-start | bytes 8519680 | tf_op jit(solution)/shard_map/all_gather | solution.py:53
  9.3 607.5 %all-gather.15.cloned.1.call-start = ((), (), s32[]{:S(2)}) async-start(), calls=%async_computation.4 | async-start | bytes 1064960 | tf_op jit(solution)/shard_map/all_gather | solution.py:79
  330.4 393.3 %all-gather.17.cloned.1.call-start = ((), (), s32[]{:S(2)}) async-start(), calls=%async_computation.5 | async-start | bytes 1064960 | tf_op jit(solution)/shard_map/all_gather | solution.py:80
  333.3 179.6 %copy-start.2 = (f32[8192]{0:T(1024)S(1)}, f32[8192]{0:T(1024)}, u32[]{:S(2)}) copy-start(f32[8192]{0:T(1024)} %param.12) | copy-start | bytes 98308
  616.8 6.0 copy-start.1
Sparse Core Ops, SparseCore 0:
  9.4 38.1 all-gather.12
  52.0 139.4 all-gather.10
  196.0 129.5 all-gather.8
  329.9 183.0 all-gather.6
  517.1 99.6 all-gather.14
  621.0 102.6 all-gather.16
where the time goes:
time: 738 us; the launch traced here: 737 us
  waiting for transfers between devices  665 us (90%)
  matrix products  22.3 us (3%)
  local copies, waits for them, and re-layouts  21.8 us (3%)
  between operations  14.3 us (2%)
  other arithmetic  14.1 us (2%)
    all_gather x1, waiting for transfers between devices, on_device(): lax.all_gather(q_weight, 'fsdp', axis=0, tiled=True)  157 us
    all_gather x1, waiting for transfers between devices, on_device(): lax.all_gather(v_weight, 'fsdp', axis=0, tiled=True)  144 us
    all_gather x1, waiting for transfers between devices, on_device(): lax.all_gather(k_weight, 'fsdp', axis=0, tiled=True)  134 us
    all_gather x1, waiting for transfers between devices, on_device(): key_piece = lax.all_gather(keys, 'fsdp', axis=1, tiled=True)  95.6 us
    all_gather x1, waiting for transfers between devices, on_device(): value_piece = lax.all_gather(values, 'fsdp', axis=1, tiled=True)  93.4 us
    all_gather x1, waiting for transfers between devices, on_device(): lax.all_gather(vision, 'img', axis=0, tiled=True)  38.2 us
    broadcast_in_dim x2, local copies, waits for them, and re-layouts, on_device(): jnp.where(allowed[:, None, :], scores.reshape(token_rows, per_group, -1),...  18 us
  transfers between devices with their start and end apart: 6, of which 6 were waited for; matrix products, arithmetic and copies ran while one was open for 7% of the time, Pallas kernels for 0%

commit v1 on v0

--- a/solution.py
+++ b/solution.py
@@ -77,7 +77,9 @@
     row_live = jnp.any(token_images, axis=1)
     score_scale = head_size ** (-0.5)
     key_piece = lax.all_gather(keys, "fsdp", axis=1, tiled=True)
-    value_piece = lax.all_gather(values, "fsdp", axis=1, tiled=True)
+    value_piece = jnp.concatenate(
+        lax.all_to_all(jnp.stack([values] * lax.axis_size("fsdp")), "fsdp", 0, 0), axis=1
+    )
     key_count = key_piece.shape[1]
     allowed = jnp.broadcast_to(token_images[:, :, None], (token_rows, images, key_count)).reshape(
         token_rows, images * key_count

time: 738 us -> 652 us (0.88)
  waiting for transfers between devices: 665 us -> 576 us
  starting transfers between devices: 0.2 us -> 9.81 us
    all_gather x1 -> x0, waiting for transfers between devices: 93.4 us -> none  [on_device(): value_piece = lax.all_gather(values, 'fsdp', axis=1, tiled=True)]
    all_to_all x0 -> x1, starting transfers between devices: none -> 9.62 us  [on_device(): lax.all_to_all(jnp.stack([values] * lax.axis_size('fsdp')), 'fsdp', 0, 0)]
  transfers between devices with their start and end apart: 6 -> 6, of which waited for: 6 -> 6; matrix products, arithmetic and copies ran while one was open for 7% -> 6% of each run, Pallas kernels for 0% -> 0%
where the time goes in v1:
time: 652 us
  waiting for transfers between devices  576 us (88%)
  local copies, waits for them, and re-layouts  22.7 us (3%)
  matrix products  18.5 us (3%)
  between operations  14.1 us (2%)
  other arithmetic  10.8 us (2%)
  starting transfers between devices  9.81 us (2%)
    all_gather x1, waiting for transfers between devices, on_device(): lax.all_gather(q_weight, 'fsdp', axis=0, tiled=True)  159 us
    all_gather x1, waiting for transfers between devices, on_device(): lax.all_gather(v_weight, 'fsdp', axis=0, tiled=True)  144 us
    all_gather x1, waiting for transfers between devices, on_device(): lax.all_gather(k_weight, 'fsdp', axis=0, tiled=True)  134 us
    all_gather x1, waiting for transfers between devices, on_device(): key_piece = lax.all_gather(keys, 'fsdp', axis=1, tiled=True)  95.6 us
    all_gather x1, waiting for transfers between devices, on_device(): lax.all_gather(vision, 'img', axis=0, tiled=True)  38.3 us
    broadcast_in_dim x2, local copies, waits for them, and re-layouts, on_device(): jnp.where(allowed[:, None, :], scores.reshape(token_rows, per_group, -1),...  18.1 us
  transfers between devices with their start and end apart: 6, of which 6 were waited for; matrix products, arithmetic and copies ran while one was open for 6% of the time, Pallas kernels for 0%

profile of v1, /device:TPU:22, one launch (start us, length us, event | category | flops | bytes accessed | tf_op | source)
XLA Modules:
  0.0 651.6 jit_solution(10841167907279179230)
XLA Ops:
  6.6 0.7 all-gather.12.cloned.1.call-update
  7.3 0.7 all-gather.10.cloned.1.call-update
  8.1 0.7 all-gather.8.cloned.1.call-update
  8.8 0.5 all-gather.6.cloned.1.call-update
  9.3 38.3 %all-gather.12.cloned.1.call-done = bf16[8,8,8192]{2,1,0:T(8,128)(2,1)} async-done(((bf16[1,8,8192]{2,1,0:T(8,128)(2,1)}), bf16[8,8,8192]{2,1,0:T(8,128)(2,1)}) %all-gather.12.cloned.1.call-update) | async-done | bytes 1048592 | tf_op jit(solution)/shard_map/all_gather | solution.py:40
  47.6 143.9 %all-gather.10.cloned.1.call-done = bf16[8192,128]{1,0:T(8,128)(2,1)} async-done(((bf16[128,128]{1,0:T(8,128)(2,1)}), bf16[8192,128]{1,0:T(8,128)(2,1)}) %all-gather.10.cloned.1.call-update) | async-done | bytes 2097168 | tf_op jit(solution)/shard_map/all_gather | solution.py:45
  191.5 134.0 %all-gather.8.cloned.1.call-done = bf16[8192,128]{1,0:T(8,128)(2,1)} async-done(((bf16[128,128]{1,0:T(8,128)(2,1)}), bf16[8192,128]{1,0:T(8,128)(2,1)}) %all-gather.8.cloned.1.call-update) | async-done | bytes 2097168 | tf_op jit(solution)/shard_map/all_gather | solution.py:44
  325.6 3.3 fusion.14
  328.9 1.3 stack.3
  330.2 9.6 %all-to-all-start = ((bf16[64,8,8,128]{3,2,1,0:T(8,128)(2,1)}), bf16[64,8,8,128]{3,2,1,0:T(8,128)(2,1)S(1)}, u32[]{:S(2)}, u32[]{:S(2)}) async-start(bf16[64,8,8,128]{3,2,1,0:T(8,128)(2,1)} %stack.3), calls=%async_computation | async-start | bytes 2097152 | tf_op jit(solution)/shard_map/all_to_all | solution.py:81
  339.9 3.2 fusion.1
  343.2 0.7 fusion.20
  344.0 0.2 fusion.23
  344.2 0.5 broadcast_in_dim.68
  344.7 0.8 copy.19
  345.5 5.7 broadcast_in_dim.70
  351.2 12.4 %broadcast_in_dim.71 = pred[1024,4096]{1,0:T(32,128)(4,1)} reshape(pred[256,4,4096]{2,1,0:T(4,128)(4,1)} %broadcast_in_dim.70) | data formatting | bytes 8388608 | tf_op jit(solution)/shard_map/jit(_where)/broadcast_in_dim | solution.py:97
  363.8 0.1 reshape.109
  364.7 2.2 all-to-all-done
  366.9 0.2 copy.18
  367.1 159.0 %all-gather.6.cloned.1.call-done = bf16[8192,512]{1,0:T(8,128)(2,1)} async-done(((bf16[128,512]{1,0:T(8,128)(2,1)}), bf16[8192,512]{1,0:T(8,128)(2,1)}) %all-gather.6.cloned.1.call-update) | async-done | bytes 8388624 | tf_op jit(solution)/shard_map/all_gather | solution.py:53
  526.1 7.0 %fusion.26 = (f32[256,512]{1,0:T(8,128)S(1)}, f32[256,512]{1,0:T(8,128)S(1)}) fusion(bf16[8192,512]{1,0:T(8,128)(2,1)} %all-gather.6.cloned.1.call-done, bf16[256,8192]{1,0:T(8,128)(2,1)} %param.11, f32[8192]{0:T(1024)S(1)} %copy-done.4, f32[256]{0:T(256)S(1)} %add_rsqrt_fusion.1), kind=kOutput, calls=%fused_computation.42 | convolution fusion | flops 2156003328 | bytes 13665280 | tf_op jit(solution)/shard_map/dot_general | solution.py:51
  533.1 0.2 mul.90
  533.3 0.3 reduce_sum.37
  533.7 0.3 mul.91
  534.0 0.1 fusion.19
  534.2 0.2 convert_element_type.32
  534.3 95.6 %all-gather.14.cloned.1.call-done = bf16[8,512,128]{2,1,0:T(8,128)(2,1)} async-done(((bf16[8,8,128]{2,1,0:T(8,128)(2,1)}), bf16[8,512,128]{2,1,0:T(8,128)(2,1)}) %all-gather.14.cloned.1.call-update) | async-done | bytes 1048592 | tf_op jit(solution)/shard_map/all_gather | solution.py:79
  629.9 5.8 fusion
  635.8 6.1 convert_reduce_fusion
  641.8 2.3 fusion.13
  644.2 0.9 convert_element_type.37
  (31 shorter events, 0.7 us)
Async XLA Ops:
  6.5 358.1 %copy-start = (f32[128]{0:T(128)S(1)}, f32[128]{0:T(128)}, u32[]{:S(2)}) copy-start(f32[128]{0:T(128)} %param.17) | copy-start | bytes 1540
  6.5 336.6 %copy-start.3 = (f32[128]{0:T(128)S(1)}, f32[128]{0:T(128)}, u32[]{:S(2)}) copy-start(f32[128]{0:T(128)} %param.18) | copy-start | bytes 1540
  6.5 337.4 %copy-start.5 = (s32[4]{0:T(128)S(1)}, s32[4]{0:T(128)}, u32[]{:S(2)}) copy-start(s32[4]{0:T(128)} %param.20) | copy-start | bytes 52
  6.5 337.4 %copy-start.2 = (s32[4,4]{1,0:T(4,128)S(1)}, s32[4,4]{1,0:T(4,128)}, u32[]{:S(2)}) copy-start(s32[4,4]{1,0:T(4,128)} %param.19) | copy-start | bytes 196
  6.5 41.1 %all-gather.12.cloned.1.call-start = ((), (), s32[]{:S(2)}) async-start(), calls=%async_computation.4 | async-start | bytes 1179648 | tf_op jit(solution)/shard_map/all_gather | solution.py:40
  7.3 184.2 %all-gather.10.cloned.1.call-start = ((), (), s32[]{:S(2)}) async-start(), calls=%async_computation.3 | async-start | bytes 2129920 | tf_op jit(solution)/shard_map/all_gather | solution.py:45
  8.0 317.5 %all-gather.8.cloned.1.call-start = ((), (), s32[]{:S(2)}) async-start(), calls=%async_computation.2 | async-start | bytes 2129920 | tf_op jit(solution)/shard_map/all_gather | solution.py:44
  8.8 517.3 %all-gather.6.cloned.1.call-start = ((), (), s32[]{:S(2)}) async-start(), calls=%async_computation.1 | async-start | bytes 8519680 | tf_op jit(solution)/shard_map/all_gather | solution.py:53
  330.2 36.7 %all-to-all-start = ((bf16[64,8,8,128]{3,2,1,0:T(8,128)(2,1)}), bf16[64,8,8,128]{3,2,1,0:T(8,128)(2,1)S(1)}, u32[]{:S(2)}, u32[]{:S(2)}) async-start(bf16[64,8,8,128]{3,2,1,0:T(8,128)(2,1)} %stack.3), calls=%async_computation | async-start | bytes 2097152 | tf_op jit(solution)/shard_map/all_to_all | solution.py:81
  339.8 290.1 %all-gather.14.cloned.1.call-start = ((), (), s32[]{:S(2)}) async-start(), calls=%async_computation.5 | async-start | bytes 1064960 | tf_op jit(solution)/shard_map/all_gather | solution.py:79
  345.5 180.6 %copy-start.4 = (f32[8192]{0:T(1024)S(1)}, f32[8192]{0:T(1024)}, u32[]{:S(2)}) copy-start(f32[8192]{0:T(1024)} %param.12) | copy-start | bytes 98308
  629.9 5.8 copy-start.1
Sparse Core Ops, SparseCore 0:
  9.4 38.1 all-gather.11
  52.1 139.4 all-gather.9
  196.0 129.5 all-gather.7
  329.9 196.1 all-gather.5
  530.3 99.6 all-gather.13
